TPU v7x, 32 devices: a whole 2x2x4 slice. The times are simulated.
32 devices in a mesh: dp: 8 (over z, y), tp: 4 (over x, core).
Axes of the slice: x: 2, y: 2, z: 4, core: 2. Of those that a mesh axis runs over, the one named last changes fastest.
Arguments:
- tokens: bfloat16 [8, 2048, 768], P('dp', 'tp'), may hold values from -6 to 6
- cotangent: bfloat16 [8, 2048, 768], P('dp', 'tp'), may hold values from -6 to 6
- tags: int32 [8], P('dp'), may hold values from 0 to 7
- tag_weight: float32 [8], replicated, may hold values from 0.25 to 4
- query_weight: bfloat16 [768, 768], P(None, 'tp'), may hold values from -0.21875 to 0.21875
- key_value_weight: bfloat16 [768, 128], replicated, may hold values from -0.21875 to 0.21875
- output_weight: bfloat16 [768, 768], P('tp'), may hold values from -1.25 to 1.25
- up_weight: bfloat16 [768, 3072], P(None, 'tp'), may hold values from -0.21875 to 0.21875
- down_weight: bfloat16 [3072, 768], P('tp'), may hold values from -0.109375 to 0.109375
- norm_gain_one: float32 [768], replicated, may hold values from 0.25 to 1.75
- norm_bias_one: float32 [768], replicated, may hold values from -1.5 to 1.5
- norm_gain_two: float32 [768], replicated, may hold values from 0.25 to 1.75
- norm_bias_two: float32 [768], replicated, may hold values from -1.5 to 1.5
Outputs:
- block_out: bfloat16 [8, 2048, 768], P('dp', 'tp')
- grad_tokens: bfloat16 [8, 2048, 768], P('dp', 'tp')
- grad_query: float32 [768, 768], P(None, 'tp')
- grad_keyval: float32 [768, 128], replicated
- grad_output: float32 [768, 768], P('tp')
- grad_upward: float32 [768, 3072], P(None, 'tp')
- grad_downward: float32 [3072, 768], P('tp')
- grad_gain_one: float32 [768], replicated
- grad_bias_one: float32 [768], replicated
- grad_gain_two: float32 [768], replicated
- grad_bias_two: float32 [768], replicated
All inputs are finite; a program needn't handle non-finite values.
Results may differ from a plain program's by a relative error of at most 0.013.
Values may be sent and summed in bfloat16 or wider, within the bound.
A program may use at most 128 MiB of HBM per device.

v0:
```python
import jax
import jax.numpy as jnp
from jax import lax
from jax.sharding import PartitionSpec as P

HD = 64
ROT = 16


def layer_norm(values, gain_vec, shift_vec):
    row_mean = jnp.mean(values, axis=-1, keepdims=True)
    centred = values - row_mean
    variance = jnp.mean(centred * centred, axis=-1, keepdims=True)
    inverse = lax.rsqrt(variance + 1e-05)
    normal = centred * inverse
    return (normal * gain_vec + shift_vec, normal, inverse)


def norm_back(scaled, normal, inverse):
    term_one = jnp.mean(scaled, axis=-1, keepdims=True)
    term_two = jnp.mean(scaled * normal, axis=-1, keepdims=True)
    return inverse * (scaled - term_one - normal * term_two)


def rot_angles(positions):
    frequencies = 10000.0 ** (-jnp.arange(0, ROT, 2, dtype=jnp.float32) / ROT)
    return positions.astype(jnp.float32)[:, None] * frequencies[None, :]


def rotate(values, angles, direction):
    half_rot = ROT // 2
    cosine = jnp.cos(angles)[:, None, :]
    sine_part = direction * jnp.sin(angles)[:, None, :]
    front_half = values[..., :half_rot]
    back_half = values[..., half_rot:ROT]
    return jnp.concatenate(
        [
            front_half * cosine - back_half * sine_part,
            back_half * cosine + front_half * sine_part,
            values[..., ROT:],
        ],
        axis=-1,
    )


def outer_sum(left, right):
    return lax.dot_general(
        left, right, (((0, 1), (0, 1)), ((), ())), preferred_element_type=jnp.float32
    )


def against(left, weight):
    return lax.dot_general(
        left, weight, (((2,), (1,)), ((), ())), preferred_element_type=jnp.float32
    )


def shards(
    tokens,
    cotangent,
    tags,
    tag_weight,
    query_weight,
    key_value_weight,
    output_weight,
    up_weight,
    down_weight,
    norm_gain_one,
    norm_bias_one,
    norm_gain_two,
    norm_bias_two,
):
    seq_dev, own_len, model_width = tokens.shape
    full_len = own_len * lax.axis_size("tp")
    heads_dev = query_weight.shape[1] // HD
    score_scale = HD ** (-0.5)
    block_rows = min(512, full_len)
    blocks = full_len // block_rows
    own_rows = tokens.astype(jnp.float32)
    full_angles = rot_angles(jnp.arange(full_len))
    tag_ids = jnp.arange(tag_weight.shape[0], dtype=jnp.int32)
    row_weight = jnp.sum(
        jnp.where(tags[:, None] == tag_ids[None, :], tag_weight[None, :], 0.0), axis=1
    )
    upstream = cotangent.astype(jnp.float32) * row_weight[:, None, None]
    all_rows = lax.all_gather(tokens, "tp", axis=1, tiled=True).astype(jnp.float32)
    grad_rows = lax.all_gather(upstream.astype(jnp.bfloat16), "tp", axis=1, tiled=True)
    normed_one, normal_all, _ = layer_norm(all_rows, norm_gain_one, norm_bias_one)
    rows_one = normed_one.astype(jnp.bfloat16)
    rows_two = (normal_all * norm_gain_two + norm_bias_two).astype(jnp.bfloat16)
    key_value_rows = jnp.dot(rows_one, key_value_weight, preferred_element_type=jnp.float32)
    key_part = rotate(key_value_rows[:, :, None, :HD], full_angles, 1.0)[:, :, 0, :]
    key_value_rows = jnp.concatenate([key_part, key_value_rows[:, :, HD:]], axis=-1).astype(
        jnp.bfloat16
    )
    key_rows = key_value_rows[:, :, :HD]
    value_rows = key_value_rows[:, :, HD:]
    query_matrix = jnp.dot(rows_one, query_weight, preferred_element_type=jnp.float32).reshape(
        seq_dev, full_len, heads_dev, HD
    )
    query_matrix = rotate(query_matrix, full_angles, 1.0).astype(jnp.bfloat16)

    def block_scores(query_block, block_start):
        block_end = block_start + block_rows
        scores = (
            jnp.einsum(
                "sqhd,skd->sqhk",
                query_block,
                key_rows[:, :block_end],
                preferred_element_type=jnp.float32,
            )
            * score_scale
        )
        allowed = jnp.arange(block_end)[None, :] <= (block_start + jnp.arange(block_rows))[:, None]
        return jnp.where(allowed[None, :, None, :], scores, -1e30)

    context_list = []
    lse_list = []
    for block_index in range(blocks):
        block_start = block_index * block_rows
        block_end = block_start + block_rows
        scores = block_scores(query_matrix[:, block_start:block_end], block_start)
        row_top = jnp.max(scores, axis=-1, keepdims=True)
        weights = jnp.exp(scores - row_top)
        row_total = jnp.sum(weights, axis=-1, keepdims=True)
        weights_low = (weights / row_total).astype(jnp.bfloat16)
        context_list.append(
            jnp.einsum(
                "sqhk,skd->sqhd",
                weights_low,
                value_rows[:, :block_end],
                preferred_element_type=jnp.float32,
            )
        )
        lse_list.append(row_top + jnp.log(row_total))
    context_full = jnp.concatenate(context_list, axis=1)
    low_context = context_full.reshape(seq_dev, full_len, heads_dev * HD).astype(jnp.bfloat16)
    attention_branch = jnp.dot(low_context, output_weight, preferred_element_type=jnp.float32)
    hidden_rows = jnp.dot(rows_two, up_weight, preferred_element_type=jnp.float32)
    middle_rows = jax.nn.gelu(hidden_rows, approximate=False).astype(jnp.bfloat16)
    feedforward_branch = jnp.dot(middle_rows, down_weight, preferred_element_type=jnp.float32)
    branch = lax.psum_scatter(
        (attention_branch + feedforward_branch).astype(jnp.bfloat16),
        "tp",
        scatter_dimension=1,
        tiled=True,
    ).astype(jnp.float32)
    block_out = (own_rows + branch).astype(jnp.bfloat16)
    grad_output = outer_sum(low_context, grad_rows)
    grad_downward = outer_sum(middle_rows, grad_rows)
    grad_context = (
        against(grad_rows, output_weight)
        .astype(jnp.bfloat16)
        .reshape(seq_dev, full_len, heads_dev, HD)
    )
    grad_middle = against(grad_rows, down_weight)
    normal_cdf = 0.5 * (1.0 + lax.erf(hidden_rows * 0.7071067811865476))
    density = jnp.exp(-0.5 * hidden_rows * hidden_rows) * 0.3989422804014327
    grad_hidden = (grad_middle * (normal_cdf + hidden_rows * density)).astype(jnp.bfloat16)
    grad_upward = outer_sum(rows_two, grad_hidden)
    norm_part_two = against(grad_hidden, up_weight)
    grad_kv_full = jnp.zeros((seq_dev, full_len, 2 * HD), jnp.float32)
    query_grad_list = []
    for block_index in range(blocks):
        block_start = block_index * block_rows
        block_end = block_start + block_rows
        query_block = query_matrix[:, block_start:block_end]
        grad_block = grad_context[:, block_start:block_end]
        scores = block_scores(query_block, block_start)
        weights = jnp.exp(scores - lse_list[block_index])
        grad_weights = jnp.einsum(
            "sqhd,skd->sqhk",
            grad_block,
            value_rows[:, :block_end],
            preferred_element_type=jnp.float32,
        )
        row_delta = jnp.sum(
            grad_block.astype(jnp.float32) * context_list[block_index], axis=-1, keepdims=True
        )
        grad_scores = (weights * (grad_weights - row_delta)).astype(jnp.bfloat16)
        query_grad_list.append(
            jnp.einsum(
                "sqhk,skd->sqhd",
                grad_scores,
                key_rows[:, :block_end],
                preferred_element_type=jnp.float32,
            )
            * score_scale
        )
        grad_keys = (
            jnp.einsum(
                "sqhk,sqhd->skd", grad_scores, query_block, preferred_element_type=jnp.float32
            )
            * score_scale
        )
        grad_values = jnp.einsum(
            "sqhk,sqhd->skd",
            weights.astype(jnp.bfloat16),
            grad_block,
            preferred_element_type=jnp.float32,
        )
        grad_kv_full = grad_kv_full.at[:, :block_end].add(
            jnp.concatenate([grad_keys, grad_values], axis=-1)
        )
    grad_queries = jnp.concatenate(query_grad_list, axis=1)
    grad_queries = (
        rotate(grad_queries, full_angles, -1.0)
        .reshape(seq_dev, full_len, heads_dev * HD)
        .astype(jnp.bfloat16)
    )
    grad_query = outer_sum(rows_one, grad_queries)
    norm_part_one = against(grad_queries, query_weight)
    key_back = rotate(grad_kv_full[:, :, None, :HD], full_angles, -1.0)[:, :, 0, :]
    keyval_part = jnp.concatenate([key_back, grad_kv_full[:, :, HD:]], axis=-1)
    low_keyval = keyval_part.astype(jnp.bfloat16)
    grad_keyval = outer_sum(rows_one, low_keyval)
    part_one = norm_part_one + against(low_keyval, key_value_weight)
    small = jnp.stack(
        [
            jnp.sum(part_one * normal_all, axis=(0, 1)),
            jnp.sum(part_one, axis=(0, 1)),
            jnp.sum(norm_part_two * normal_all, axis=(0, 1)),
            jnp.sum(norm_part_two, axis=(0, 1)),
        ]
    )
    scaled = lax.psum_scatter(
        (part_one * norm_gain_one + norm_part_two * norm_gain_two).astype(jnp.bfloat16),
        "tp",
        scatter_dimension=1,
        tiled=True,
    ).astype(jnp.float32)
    _, normal_own, inverse_own = layer_norm(own_rows, norm_gain_one, norm_bias_one)
    grad_tokens = upstream + norm_back(scaled, normal_own, inverse_own)
    grad_query, grad_output, grad_upward, grad_downward = [
        v.astype(jnp.float32)
        for v in lax.psum(
            tuple(
                (
                    v.astype(jnp.bfloat16)
                    for v in (grad_query, grad_output, grad_upward, grad_downward)
                )
            ),
            "dp",
        )
    ]
    tail = lax.psum(
        jnp.concatenate([grad_keyval.reshape(-1), small.reshape(-1)]).reshape(-1, 128), ("dp", "tp")
    ).reshape(-1)
    grad_keyval, small = (
        tail[: grad_keyval.size].reshape(grad_keyval.shape),
        tail[grad_keyval.size :].reshape(small.shape),
    )
    grad_gain_one, grad_bias_one, grad_gain_two, grad_bias_two = small
    return (
        block_out,
        grad_tokens.astype(jnp.bfloat16),
        grad_query,
        grad_keyval,
        grad_output,
        grad_upward,
        grad_downward,
        grad_gain_one,
        grad_bias_one,
        grad_gain_two,
        grad_bias_two,
    )


def solution(mesh):
    in_specs = (
        P("dp", "tp", None),
        P("dp", "tp", None),
        P("dp"),
        P(),
        P(None, "tp"),
        P(),
        P("tp", None),
        P(None, "tp"),
        P("tp", None),
        P(),
        P(),
        P(),
        P(),
    )
    out_specs = (
        P("dp", "tp", None),
        P("dp", "tp", None),
        P(None, "tp"),
        P(),
        P("tp", None),
        P(None, "tp"),
        P("tp", None),
        P(),
        P(),
        P(),
        P(),
    )
    return jax.shard_map(shards, mesh=mesh, in_specs=in_specs, out_specs=out_specs, check_vma=False)
```

profile of v0, /device:TPU:0, one launch (start us, length us, event | category | flops | bytes accessed | tf_op | source)
XLA Modules:
  0.0 513.2 jit_solution(20159249226310110)
XLA Ops:
  9.9 2.8 fusion.102
  17.0 23.9 %all-gather.3.cloned.1.call-done = bf16[1,2048,768]{2,1,0:T(8,128)(2,1)} async-done(((bf16[1,512,768]{2,1,0:T(8,128)(2,1)}), bf16[1,2048,768]{2,1,0:T(8,128)(2,1)}) %all-gather.3.cloned.1.call-update) | async-done | bytes 3145744 | tf_op jit(solution)/shard_map/all_gather | solution.py:86
  40.9 2.5 convert_reduce_fusion
  43.4 2.9 fusion.17
  61.7 6.2 %fusion.10 = (f32[512,3]{0,1:T(4,128)S(1)}, f32[512,3,2048]{2,0,1:T(8,128)}) fusion(pred[512,2048]{1,0:T(8,128)(4,1)S(1)} %iota_compare_fusion, bf16[1,2048,1,48]{1,3,2,0:T(8,128)(2,1)S(1)} %slice.387, bf16[1,2048,1,8]{1,3,2,0:T(8,128)(2,1)S(1)} %get-tuple-element.92, bf16[1,2048,1,8]{1,3,2,0:T(8,128)(2,1)S(1)} %get-tuple-element.91, ...), kind=kOutput, calls=%fused_computation.25 | convolution fusion | flops 412875264 | bytes 14096384 | tf_op jit(solution)/shard_map/sqhd,skd->sqhk/dot_general | solution.py:106
  70.5 6.9 %fusion = f32[512,3]{0,1:T(4,128)S(1)} fusion(f32[512,3,2048]{2,0,1:T(8,128)} %get-tuple-element.109, f32[512,3]{0,1:T(4,128)S(1)} %get-tuple-element.108, pred[512,2048]{1,0:T(8,128)(4,1)S(1)} %iota_compare_fusion), kind=kLoop, calls=%fused_computation.6 | loop fusion | flops 12581376 | bytes 13643776 | tf_op jit(solution)/shard_map/reduce_sum | solution.py:125
  78.6 3.1 fusion.194
  82.2 2.9 fusion.193
  86.2 4.8 fusion.192
  91.0 3.1 fusion.71
  94.2 7.3 %fusion.80 = f32[1,2048,64]{1,2,0:T(8,128)} fusion(f32[512,3,2048]{2,0,1:T(8,128)} %get-tuple-element.109, f32[512,3]{0,1:T(4,128)S(1)} %copy-done.50, pred[512,2048]{1,0:T(8,128)(4,1)S(1)} %iota_compare_fusion, bf16[1,2048,3,64]{1,3,2,0:T(8,128)(2,1)S(1)} %bitcast.290), kind=kOutput, calls=%fused_computation.113 | convolution fusion | flops 415236096 | bytes 14360576 | tf_op jit(solution)/shard_map/sqhk,sqhd->skd/dot_general | solution.py:196
  101.6 2.0 fusion.132
  104.4 4.6 multiply_convert_fusion
  109.1 2.0 fusion.115
  117.3 2.4 multiply_convert_fusion.2
  123.2 2.5 multiply_convert_fusion.1
  130.1 17.6 %fusion.20 = (bf16[2048,768]{1,0:T(8,128)(2,1)}, f32[2048,768]{1,0:T(8,128)S(1)}) fusion(bf16[768,768]{1,0:T(8,128)(2,1)S(1)} %copy-done, bf16[1,2048,768]{2,1,0:T(8,128)(2,1)S(1)} %copy-done.3, f32[768]{0:T(1024)S(1)} %copy-done.59, f32[768]{0:T(1024)S(1)} %copy-done.55, f32[2048]{0:T(1024)S(1)} %copy-done.40, f32[2048]{0:T(1024)S(1)} %broadcast_multiply_fusion.1), kind=kOutput, calls=%fused_computation.35 | convolution fusion | flops 2527592448 | bytes 13785088 | tf_op jit(solution)/shard_map/dot_general | solution.py:139
  147.7 5.2 %fusion.26 = bf16[2048,768]{1,0:T(8,128)(2,1)S(1)} fusion(f32[2048,768]{1,0:T(8,128)S(1)} %get-tuple-element.112, bf16[768,768]{1,0:T(8,128)(2,1)S(1)} %copy-done.58, bf16[1,2048,768]{2,1,0:T(8,128)(2,1)S(1)} %copy-done.56), kind=kOutput, calls=%fused_computation.41 | convolution fusion | flops 2431647744 | bytes 13762560 | tf_op jit(solution)/shard_map/dot_general | solution.py:53
  152.9 2.7 fusion.197
  158.8 3.0 fusion.15
  161.8 2.9 fusion.188
  165.8 7.1 %convolution_convert_fusion = bf16[768,768]{1,0:T(8,128)(2,1)} fusion(bf16[2048,768]{1,0:T(8,128)(2,1)} %copy-done.61, bf16[1,2048,768]{2,1,0:T(8,128)(2,1)} %all-gather.3.cloned.1.call-done, f32[768]{0:T(1024)S(1)} %copy-done.59, f32[768]{0:T(1024)S(1)} %copy-done.55, f32[2048]{0:T(1024)S(1)} %copy-done.40, f32[2048]{0:T(1024)S(1)} %broadcast_multiply_fusion.1), kind=kOutput, calls=%fused_computation.143 | convolution fusion | flops 2425946112 | bytes 7493632 | tf_op jit(solution)/shard_map/dot_general | solution.py:47
  173.0 3.7 fusion.104
  180.6 4.9 fusion.195
  185.5 2.7 fusion.65
  188.8 102.7 %all-reduce.5.cloned.1.call-done = f32[792,128]{1,0:T(8,128)} async-done(((f32[792,128]{1,0:T(8,128)}), f32[792,128]{1,0:T(8,128)}) %all-reduce.5.cloned.1.call-update) | async-done | bytes 405520 | tf_op jit(solution)/shard_map/psum | solution.py:246
  294.7 127.7 %all-reduce.7.cloned.1.call-done = (bf16[768,192]{0,1:T(8,128)(2,1)}, bf16[192,768]{1,0:T(8,128)(2,1)}, bf16[768,768]{1,0:T(8,128)(2,1)}, bf16[768,768]{1,0:T(8,128)(2,1)}) async-done(((bf16[768,192]{0,1:T(8,128)(2,1)}, bf16[192,768]{1,0:T(8,128)(2,1)}, bf16[768,768]{1,0:T(8,128)(2,1)}, bf16[768,768]{1,0:T(8,128)(2,1)}), (bf16[768,192]{0,1:T(8,128)(2,1)}, bf16[192,768]{1,0:T(8,128)(2,1)}, ...) | async-done | bytes 2949136 | tf_op jit(solution)/shard_map/psum | solution.py:236
  426.1 2.8 convert_element_type.267
  428.9 2.9 convert_element_type.269
  431.8 29.9 %reduce-scatter.5.cloned.1.call-done = bf16[1,512,768]{2,1,0:T(8,128)(2,1)} async-done(((bf16[1,2048,768]{2,1,0:T(8,128)(2,1)}), bf16[1,512,768]{2,1,0:T(8,128)(2,1)}) %reduce-scatter.5.cloned.1.call-update) | async-done | bytes 786448 | tf_op jit(solution)/shard_map/reduce_scatter | solution.py:226
  463.6 38.7 %reduce-scatter.3.cloned.1.call-done = bf16[1,512,768]{2,1,0:T(8,128)(2,1)} async-done(((bf16[1,2048,768]{2,1,0:T(8,128)(2,1)}), bf16[1,512,768]{2,1,0:T(8,128)(2,1)}) %reduce-scatter.3.cloned.1.call-update) | async-done | bytes 786448 | tf_op jit(solution)/shard_map/reduce_scatter | solution.py:142
  502.2 3.8 fusion.93
  (253 shorter events, 58.7 us)
Async XLA Ops:
  7.2 122.1 %copy-start = (bf16[768,768]{1,0:T(8,128)(2,1)S(1)}, bf16[768,768]{1,0:T(8,128)(2,1)}, u32[]{:S(2)}) copy-start(bf16[768,768]{1,0:T(8,128)(2,1)} %param.30) | copy-start | bytes 3538948
  7.2 39.8 %copy-start.46 = (f32[768]{0:T(1024)S(1)}, f32[768]{0:T(1024)}, u32[]{:S(2)}) copy-start(f32[768]{0:T(1024)} %param.32) | copy-start | bytes 9220
  7.2 39.8 %copy-start.54 = (f32[768]{0:T(1024)S(1)}, f32[768]{0:T(1024)}, u32[]{:S(2)}) copy-start(f32[768]{0:T(1024)} %param.33) | copy-start | bytes 9220
  7.2 33.7 %all-gather.3.cloned.1.call-start = ((), (), s32[]{:S(2)}) async-start(), calls=%async_computation.2 | async-start | bytes 3932160 | tf_op jit(solution)/shard_map/all_gather | solution.py:86
  7.9 83.1 %all-gather.5.cloned.1.call-start = ((), (), s32[]{:S(2)}) async-start(), calls=%async_computation.4 | async-start | bytes 3932160 | tf_op jit(solution)/shard_map/all_gather | solution.py:87
  12.7 278.8 %all-reduce.5.cloned.1.call-start = ((), (), s32[]{:S(2)}) async-start(), calls=%async_computation.6 | async-start | bytes 811008 | tf_op jit(solution)/shard_map/psum | solution.py:246
  12.8 28.1 %copy-start.51 = (f32[8]{0:T(128)}, f32[8]{0:T(128)S(1)}, u32[]{:S(2)}) copy-start(f32[8]{0:T(128)S(1)} %multiply_power_fusion) | copy-start | bytes 100
  17.0 35.2 %copy-start.18 = (f32[2048,8]{0,1:T(8,128)}, f32[2048,8]{0,1:T(8,128)S(1)}, u32[]{:S(2)}) copy-start(f32[2048,8]{0,1:T(8,128)S(1)} %get-tuple-element.99) | copy-start | bytes 196612
  17.0 31.5 %copy-start.20 = (bf16[768,128]{1,0:T(8,128)(2,1)S(1)}, bf16[768,128]{1,0:T(8,128)(2,1)}, u32[]{:S(2)}) copy-start(bf16[768,128]{1,0:T(8,128)(2,1)} %param.28) | copy-start | bytes 589828
  50.9 10.8 %copy-start.25 = (bf16[1,2048,1,8]{1,3,2,0:T(8,128)(2,1)}, bf16[1,2048,1,8]{1,3,2,0:T(8,128)(2,1)S(1)}, u32[]{:S(2)}) copy-start(bf16[1,2048,1,8]{1,3,2,0:T(8,128)(2,1)S(1)} %get-tuple-element.91) | copy-start | bytes 98308
  50.9 10.8 %copy-start.27 = (bf16[1,2048,1,8]{1,3,2,0:T(8,128)(2,1)}, bf16[1,2048,1,8]{1,3,2,0:T(8,128)(2,1)S(1)}, u32[]{:S(2)}) copy-start(bf16[1,2048,1,8]{1,3,2,0:T(8,128)(2,1)S(1)} %get-tuple-element.92) | copy-start | bytes 98308
  50.9 10.8 %copy-start.12 = (bf16[1,2048,1,48]{1,3,2,0:T(8,128)(2,1)}, bf16[1,2048,1,48]{1,3,2,0:T(8,128)(2,1)S(1)}, u32[]{:S(2)}) copy-start(bf16[1,2048,1,48]{1,3,2,0:T(8,128)(2,1)S(1)} %slice.387) | copy-start | bytes 589828
  52.4 7.3 %copy-start.14 = (bf16[1,2048,64]{1,2,0:T(8,128)(2,1)}, bf16[1,2048,64]{1,2,0:T(8,128)(2,1)S(1)}, u32[]{:S(2)}) copy-start(bf16[1,2048,64]{1,2,0:T(8,128)(2,1)S(1)} %fusion.184) | copy-start | bytes 786436
  57.1 21.4 %copy-start.10 = (f32[512,3,1024]{2,0,1:T(8,128)}, f32[512,3,1024]{2,0,1:T(8,128)S(1)}, u32[]{:S(2)}) copy-start(f32[512,3,1024]{2,0,1:T(8,128)S(1)} %get-tuple-element.105) | copy-start | bytes 18874372
  61.7 7.4 %copy-start.1 = (f32[512,3,1536]{2,0,1:T(8,128)}, f32[512,3,1536]{2,0,1:T(8,128)S(1)}, u32[]{:S(2)}) copy-start(f32[512,3,1536]{2,0,1:T(8,128)S(1)} %get-tuple-element.107) | copy-start | bytes 28311556
  70.4 8.1 %copy-start.16 = (bf16[1,2048,128]{1,2,0:T(8,128)(2,1)S(1)}, bf16[1,2048,128]{1,2,0:T(8,128)(2,1)}, u32[]{:S(2)}) copy-start(bf16[1,2048,128]{1,2,0:T(8,128)(2,1)} %get-tuple-element.102) | copy-start | bytes 1572868
  70.4 11.3 %slice-start = ((s8[9437184]{0:T(1024)(128)(4,1)}), s8[1048576]{0:T(1024)(128)(4,1)S(1)}, s32[]{:S(2)}) async-start(s8[9437184]{0:T(1024)(128)(4,1)} %bitcast.278), calls=%async_computation.8 | async-start | bytes 2097152
  94.1 7.4 %copy-start.8 = (f32[512,3,512]{0,2,1:T(8,128)S(1)}, f32[512,3,512]{0,2,1:T(8,128)}, u32[]{:S(2)}) copy-start(f32[512,3,512]{0,2,1:T(8,128)} %copy-done.7) | copy-start | bytes 9437188
  94.2 7.4 %copy-start.17 = (bf16[1,2048,128]{1,2,0:T(8,128)(2,1)S(1)}, bf16[1,2048,128]{1,2,0:T(8,128)(2,1)}, u32[]{:S(2)}) copy-start(bf16[1,2048,128]{1,2,0:T(8,128)(2,1)} %get-tuple-element.102) | copy-start | bytes 1572868
  94.2 7.4 %copy-start.43 = (f32[512,3]{0,1:T(4,128)S(1)}, f32[512,3]{0,1:T(4,128)}, u32[]{:S(2)}) copy-start(f32[512,3]{0,1:T(4,128)} %copy-done.42) | copy-start | bytes 18436
  94.2 7.4 %copy-start.45 = (f32[512,3]{0,1:T(4,128)S(1)}, f32[512,3]{0,1:T(4,128)}, u32[]{:S(2)}) copy-start(f32[512,3]{0,1:T(4,128)} %copy-done.44) | copy-start | bytes 18436
  94.2 7.4 %copy-start.62 = (f32[512,3,64]{0,2,1:T(8,128)S(1)}, f32[512,3,64]{0,2,1:T(8,128)}, u32[]{:S(2)}) copy-start(f32[512,3,64]{0,2,1:T(8,128)} %get-tuple-element.118) | copy-start | bytes 1179652
  94.2 7.4 %copy-start.63 = (f32[512,3,64]{0,2,1:T(8,128)S(1)}, f32[512,3,64]{0,2,1:T(8,128)}, u32[]{:S(2)}) copy-start(f32[512,3,64]{0,2,1:T(8,128)} %get-tuple-element.116) | copy-start | bytes 1179652
  94.2 7.4 %copy-start.64 = (f32[512,3,64]{0,2,1:T(8,128)S(1)}, f32[512,3,64]{0,2,1:T(8,128)}, u32[]{:S(2)}) copy-start(f32[512,3,64]{0,2,1:T(8,128)} %get-tuple-element.114) | copy-start | bytes 1179652
  94.2 9.4 %slice-start.9 = ((s8[12582912]{0:T(1024)(128)(4,1)}), s8[4194304]{0:T(1024)(128)(4,1)S(1)}, s32[]{:S(2)}) async-start(s8[12582912]{0:T(1024)(128)(4,1)} %bitcast.284), calls=%async_computation.17 | async-start | bytes 8388608
  94.2 9.4 %slice-start.10 = ((s8[12582912]{0:T(1024)(128)(4,1)}), s8[4194304]{0:T(1024)(128)(4,1)S(1)}, s32[]{:S(2)}) async-start(s8[12582912]{0:T(1024)(128)(4,1)} %bitcast.284), calls=%async_computation.18 | async-start | bytes 8388608
  130.1 17.6 %copy-start.56 = (bf16[1,2048,768]{2,1,0:T(8,128)(2,1)S(1)}, bf16[1,2048,768]{2,1,0:T(8,128)(2,1)}, u32[]{:S(2)}) copy-start(bf16[1,2048,768]{2,1,0:T(8,128)(2,1)} %all-gather.5.cloned.1.call-done) | copy-start | bytes 9437188
  130.1 17.6 %copy-start.58 = (bf16[768,768]{1,0:T(8,128)(2,1)S(1)}, bf16[768,768]{1,0:T(8,128)(2,1)}, u32[]{:S(2)}) copy-start(bf16[768,768]{1,0:T(8,128)(2,1)} %param.31) | copy-start | bytes 3538948
  165.5 257.0 %all-reduce.7.cloned.1.call-start = ((), (), s32[]{:S(2)}) async-start(), calls=%async_computation.7 | async-start | bytes 5898240 | tf_op jit(solution)/shard_map/psum | solution.py:236
  179.7 282.0 %reduce-scatter.5.cloned.1.call-start = ((), (), s32[]{:S(2)}) async-start(), calls=%async_computation.5 | async-start | bytes 3932160 | tf_op jit(solution)/shard_map/reduce_scatter | solution.py:226
  180.3 321.9 %reduce-scatter.3.cloned.1.call-start = ((), (), s32[]{:S(2)}) async-start(), calls=%async_computation.3 | async-start | bytes 3932160 | tf_op jit(solution)/shard_map/reduce_scatter | solution.py:142
  188.3 314.0 %copy-start.11 = (bf16[1,512,768]{2,1,0:T(8,128)(2,1)S(1)}, bf16[1,512,768]{2,1,0:T(8,128)(2,1)}, u32[]{:S(2)}) copy-start(bf16[1,512,768]{2,1,0:T(8,128)(2,1)} %param.24) | copy-start | bytes 2359300
  (53 other events, 179.6 us)
Sparse Core Ops, SparseCore 0:
  9.6 31.2 all-gather.2
  43.0 28.6 all-gather.4
  165.6 125.9 all-reduce.4
  296.6 125.8 all-reduce.6
  424.8 36.7 reduce-scatter.4
  464.2 37.9 reduce-scatter.2
where the time goes:
time: 517 us; the launch traced here: 513 us
  waiting for transfers between devices  324 us (63%)
  matrix products  111 us (21%)
  other arithmetic  49.1 us (9%)
  between operations  16.2 us (3%)
  local copies, waits for them, and re-layouts  11.6 us (2%)
    psum x1, waiting for transfers between devices, shards(): lax.psum(tuple((v.astype(jnp.bfloat16) for v in (grad_query, grad_output,...  128 us
    psum x1, waiting for transfers between devices, shards(): lax.psum(jnp.concatenate([grad_keyval.reshape(-1), small.reshape(-1)]).re...  103 us
    reduce_scatter x1, waiting for transfers between devices, shards(): lax.psum_scatter((attention_branch + feedforward_branch).astype(jnp.bfloa...  38.7 us
    reduce_scatter x1, waiting for transfers between devices, shards(): lax.psum_scatter((part_one * norm_gain_one + norm_part_two * norm_gain_tw...  29.9 us
    all_gather x1, waiting for transfers between devices, shards(): lax.all_gather(tokens, 'tp', axis=1, tiled=True).astype(jnp.float32)  23.9 us
    dot_general x1, matrix products, shards(): jnp.dot(rows_two, up_weight, preferred_element_type=jnp.float32)  17.6 us
    dot_general x5, matrix products, against(): lax.dot_general(left, weight, (((2,), (1,)), ((), ())), preferred_element...  15 us
    dot_general x5, matrix products, outer_sum(): lax.dot_general(left, right, (((0, 1), (0, 1)), ((), ())), preferred_elem...  14.9 us
  transfers between devices with their start and end apart: 6, of which 5 were waited for; matrix products, arithmetic and copies ran while one was open for 17% of the time, Pallas kernels for 0%

commit v1 on v0

--- a/solution.py
+++ b/solution.py
@@ -243,7 +243,11 @@
             "dp",
         )
     ]
-    tail = lax.psum(
+
+    def spots_use(x_local, lane_axis):
+        return lax.all_gather(x_local, lane_axis).sum(axis=0)
+
+    tail = spots_use(
         jnp.concatenate([grad_keyval.reshape(-1), small.reshape(-1)]).reshape(-1, 128), ("dp", "tp")
     ).reshape(-1)
     grad_keyval, small = (

time: 517 us -> 487 us (0.942)
  waiting for transfers between devices: 324 us -> 292 us
  other arithmetic: 49.1 us -> 54.4 us
    psum x1 -> x0, waiting for transfers between devices: 103 us -> none  [shards(): lax.psum(jnp.concatenate([grad_keyval.reshape(-1), small.reshape(-1)]).re...]
    all_gather x0 -> x1, waiting for transfers between devices: none -> 97.3 us  [spots_use(): return lax.all_gather(x_local, lane_axis).sum(axis=0)]
    psum x1, waiting for transfers between devices: 128 us -> 102 us  [shards(): lax.psum(tuple((v.astype(jnp.bfloat16) for v in (grad_query, grad_output,...]
    reduce_sum x0 -> x1, other arithmetic: none -> 5.3 us  [spots_use(): return lax.all_gather(x_local, lane_axis).sum(axis=0)]
  transfers between devices with their start and end apart: 6 -> 6, of which waited for: 5 -> 5; matrix products, arithmetic and copies ran while one was open for 17% -> 19% of each run, Pallas kernels for 0% -> 0%
where the time goes in v1:
time: 487 us; the launch traced here: 483 us
  waiting for transfers between devices  292 us (60%)
  matrix products  111 us (23%)
  other arithmetic  54.4 us (11%)
  between operations  16.3 us (3%)
  local copies, waits for them, and re-layouts  8.89 us (2%)
    psum x1, waiting for transfers between devices, shards(): lax.psum(tuple((v.astype(jnp.bfloat16) for v in (grad_query, grad_output,...  102 us
    all_gather x1, waiting for transfers between devices, spots_use(): return lax.all_gather(x_local, lane_axis).sum(axis=0)  97.3 us
    reduce_scatter x1, waiting for transfers between devices, shards(): lax.psum_scatter((attention_branch + feedforward_branch).astype(jnp.bfloa...  38.5 us
    reduce_scatter x1, waiting for transfers between devices, shards(): lax.psum_scatter((part_one * norm_gain_one + norm_part_two * norm_gain_tw...  30 us
    all_gather x1, waiting for transfers between devices, shards(): lax.all_gather(tokens, 'tp', axis=1, tiled=True).astype(jnp.float32)  23.9 us
    dot_general x1, matrix products, shards(): jnp.dot(rows_two, up_weight, preferred_element_type=jnp.float32)  16.3 us
    dot_general x5, matrix products, against(): lax.dot_general(left, weight, (((2,), (1,)), ((), ())), preferred_element...  16.2 us
    dot_general x5, matrix products, outer_sum(): lax.dot_general(left, right, (((0, 1), (0, 1)), ((), ())), preferred_elem...  14.1 us
  transfers between devices with their start and end apart: 6, of which 5 were waited for; matrix products, arithmetic and copies ran while one was open for 19% of the time, Pallas kernels for 0%

profile of v1, /device:TPU:0, one launch (start us, length us, event | category | flops | bytes accessed | tf_op | source)
XLA Modules:
  0.0 483.0 jit_solution(11907704233770937463)
XLA Ops:
  9.9 2.8 fusion.102
  17.0 23.9 %all-gather.4.cloned.1.call-done = bf16[1,2048,768]{2,1,0:T(8,128)(2,1)} async-done(((bf16[1,512,768]{2,1,0:T(8,128)(2,1)}), bf16[1,2048,768]{2,1,0:T(8,128)(2,1)}) %all-gather.4.cloned.1.call-update) | async-done | bytes 3145744 | tf_op jit(solution)/shard_map/all_gather | solution.py:86
  40.9 2.5 convert_reduce_fusion
  43.4 2.9 fusion.17
  61.8 6.3 %fusion.10 = (f32[512,3]{0,1:T(4,128)S(1)}, f32[512,3,2048]{2,0,1:T(8,128)}) fusion(pred[512,2048]{1,0:T(8,128)(4,1)S(1)} %iota_compare_fusion, bf16[1,2048,1,48]{1,3,2,0:T(8,128)(2,1)S(1)} %slice.387, bf16[1,2048,1,8]{1,3,2,0:T(8,128)(2,1)S(1)} %get-tuple-element.92, bf16[1,2048,1,8]{1,3,2,0:T(8,128)(2,1)S(1)} %get-tuple-element.91, ...), kind=kOutput, calls=%fused_computation.25 | convolution fusion | flops 412875264 | bytes 14096384 | tf_op jit(solution)/shard_map/sqhd,skd->sqhk/dot_general | solution.py:106
  70.6 6.9 %fusion = f32[512,3]{0,1:T(4,128)S(1)} fusion(f32[512,3,2048]{2,0,1:T(8,128)} %get-tuple-element.109, f32[512,3]{0,1:T(4,128)S(1)} %get-tuple-element.108, pred[512,2048]{1,0:T(8,128)(4,1)S(1)} %iota_compare_fusion), kind=kLoop, calls=%fused_computation.6 | loop fusion | flops 12581376 | bytes 13643776 | tf_op jit(solution)/shard_map/reduce_sum | solution.py:125
  78.7 3.4 fusion.194
  82.3 2.9 fusion.193
  86.4 4.8 fusion.192
  91.2 3.1 fusion.71
  94.4 7.3 %fusion.80 = f32[1,2048,64]{1,2,0:T(8,128)} fusion(f32[512,3,2048]{2,0,1:T(8,128)} %get-tuple-element.109, f32[512,3]{0,1:T(4,128)S(1)} %copy-done.54, pred[512,2048]{1,0:T(8,128)(4,1)S(1)} %iota_compare_fusion, bf16[1,2048,3,64]{1,3,2,0:T(8,128)(2,1)S(1)} %bitcast.290), kind=kOutput, calls=%fused_computation.113 | convolution fusion | flops 415236096 | bytes 14360576 | tf_op jit(solution)/shard_map/sqhk,sqhd->skd/dot_general | solution.py:196
  104.5 4.4 multiply_convert_fusion
  117.2 2.4 multiply_convert_fusion.2
  123.1 2.5 multiply_convert_fusion.1
  131.9 16.3 %fusion.20 = (bf16[2048,768]{1,0:T(8,128)(2,1)S(1)}, f32[2048,768]{1,0:T(8,128)S(1)}) fusion(bf16[768,768]{1,0:T(8,128)(2,1)S(1)} %copy-done, bf16[1,2048,768]{2,1,0:T(8,128)(2,1)S(1)} %copy-done.3, f32[768]{0:T(1024)S(1)} %copy-done.63, f32[768]{0:T(1024)S(1)} %copy-done.59, f32[2048]{0:T(1024)S(1)} %copy-done.43, f32[2048]{0:T(1024)S(1)} %broadcast_multiply_fusion.1), kind=kOutput, calls=%fused_computation.35 | convolution fusion | flops 2527592448 | bytes 13785088 | tf_op jit(solution)/shard_map/dot_general | solution.py:139
  148.2 5.4 %fusion.26 = bf16[2048,768]{1,0:T(8,128)(2,1)S(1)} fusion(f32[2048,768]{1,0:T(8,128)S(1)} %get-tuple-element.112, bf16[768,768]{1,0:T(8,128)(2,1)S(1)} %copy-done.62, bf16[1,2048,768]{2,1,0:T(8,128)(2,1)S(1)} %copy-done.61), kind=kOutput, calls=%fused_computation.41 | convolution fusion | flops 2431647744 | bytes 13762560 | tf_op jit(solution)/shard_map/dot_general | solution.py:53
  153.6 4.3 convolution_convert_fusion
  157.9 3.7 fusion.104
  165.5 2.7 fusion.197
  168.2 2.9 fusion.15
  171.2 2.8 fusion.188
  174.3 4.9 %fusion.195 = f32[2048,768]{1,0:T(8,128)S(1)} fusion(bf16[2048,768]{1,0:T(8,128)(2,1)} %copy-done.64, bf16[768,768]{1,0:T(8,128)(2,1)} %param.31), kind=kOutput, calls=%fused_computation.293 | convolution fusion | flops 2415919104 | bytes 10616832 | tf_op jit(solution)/shard_map/dot_general | solution.py:141
  179.3 2.7 fusion.65
  182.1 3.0 convolution_bitcast_fusion
  186.5 101.8 %all-reduce.4.cloned.1.call-done = (bf16[768,192]{0,1:T(8,128)(2,1)}, bf16[192,768]{1,0:T(8,128)(2,1)}, bf16[768,768]{1,0:T(8,128)(2,1)}, bf16[768,768]{1,0:T(8,128)(2,1)}) async-done(((bf16[768,192]{0,1:T(8,128)(2,1)}, bf16[192,768]{1,0:T(8,128)(2,1)}, bf16[768,768]{1,0:T(8,128)(2,1)}, bf16[768,768]{1,0:T(8,128)(2,1)}), (bf16[768,192]{0,1:T(8,128)(2,1)}, bf16[192,768]{1,0:T(8,128)(2,1)}, ...) | async-done | bytes 2949136 | tf_op jit(solution)/shard_map/psum | solution.py:236
  292.0 2.8 convert_element_type.267
  294.8 2.9 convert_element_type.269
  297.7 30.0 %reduce-scatter.5.cloned.1.call-done = bf16[1,512,768]{2,1,0:T(8,128)(2,1)} async-done(((bf16[1,2048,768]{2,1,0:T(8,128)(2,1)}), bf16[1,512,768]{2,1,0:T(8,128)(2,1)}) %reduce-scatter.5.cloned.1.call-update) | async-done | bytes 786448 | tf_op jit(solution)/shard_map/reduce_scatter | solution.py:226
  329.6 38.5 %reduce-scatter.3.cloned.1.call-done = bf16[1,512,768]{2,1,0:T(8,128)(2,1)} async-done(((bf16[1,2048,768]{2,1,0:T(8,128)(2,1)}), bf16[1,512,768]{2,1,0:T(8,128)(2,1)}) %reduce-scatter.3.cloned.1.call-update) | async-done | bytes 786448 | tf_op jit(solution)/shard_map/reduce_scatter | solution.py:142
  368.1 3.8 fusion.93
  371.9 97.3 %all-gather.8.cloned.1.call-done = f32[32,792,128]{2,1,0:T(8,128)} async-done(((f32[1,792,128]{2,1,0:T(8,128)}), f32[32,792,128]{2,1,0:T(8,128)}) %all-gather.8.cloned.1.call-update) | async-done | bytes 12976144 | tf_op jit(solution)/shard_map/all_gather | solution.py:248
  469.3 5.3 %reduce_sum.199 = f32[792,128]{1,0:T(8,128)S(1)} reduce(f32[32,792,128]{2,1,0:T(8,128)} %all-gather.8.cloned.1.call-done, f32[]{:T(128)} %constant.169.clone.1), dimensions={0}, to_apply=%region_26.27 | reduce | flops 3142656 | bytes 13381636 | tf_op jit(solution)/shard_map/reduce_sum | solution.py:248
  (264 shorter events, 59.4 us)
Async XLA Ops:
  7.2 124.6 %copy-start = (bf16[768,768]{1,0:T(8,128)(2,1)S(1)}, bf16[768,768]{1,0:T(8,128)(2,1)}, u32[]{:S(2)}) copy-start(bf16[768,768]{1,0:T(8,128)(2,1)} %param.30) | copy-start | bytes 3538948
  7.2 39.8 %copy-start.50 = (f32[768]{0:T(1024)S(1)}, f32[768]{0:T(1024)}, u32[]{:S(2)}) copy-start(f32[768]{0:T(1024)} %param.32) | copy-start | bytes 9220
  7.2 39.8 %copy-start.58 = (f32[768]{0:T(1024)S(1)}, f32[768]{0:T(1024)}, u32[]{:S(2)}) copy-start(f32[768]{0:T(1024)} %param.33) | copy-start | bytes 9220
  7.2 33.7 %all-gather.4.cloned.1.call-start = ((), (), s32[]{:S(2)}) async-start(), calls=%async_computation.2 | async-start | bytes 3932160 | tf_op jit(solution)/shard_map/all_gather | solution.py:86
  7.9 83.2 %all-gather.6.cloned.1.call-start = ((), (), s32[]{:S(2)}) async-start(), calls=%async_computation.4 | async-start | bytes 3932160 | tf_op jit(solution)/shard_map/all_gather | solution.py:87
  12.7 275.6 %all-reduce.4.cloned.1.call-start = ((), (), s32[]{:S(2)}) async-start(), calls=%async_computation.7 | async-start | bytes 5898240 | tf_op jit(solution)/shard_map/psum | solution.py:236
  12.8 28.1 %copy-start.55 = (f32[8]{0:T(128)}, f32[8]{0:T(128)S(1)}, u32[]{:S(2)}) copy-start(f32[8]{0:T(128)S(1)} %multiply_power_fusion) | copy-start | bytes 100
  17.0 35.3 %copy-start.18 = (f32[2048,8]{0,1:T(8,128)}, f32[2048,8]{0,1:T(8,128)S(1)}, u32[]{:S(2)}) copy-start(f32[2048,8]{0,1:T(8,128)S(1)} %get-tuple-element.99) | copy-start | bytes 196612
  17.0 31.6 %copy-start.20 = (bf16[768,128]{1,0:T(8,128)(2,1)S(1)}, bf16[768,128]{1,0:T(8,128)(2,1)}, u32[]{:S(2)}) copy-start(bf16[768,128]{1,0:T(8,128)(2,1)} %param.28) | copy-start | bytes 589828
  51.0 10.8 %copy-start.25 = (bf16[1,2048,1,8]{1,3,2,0:T(8,128)(2,1)}, bf16[1,2048,1,8]{1,3,2,0:T(8,128)(2,1)S(1)}, u32[]{:S(2)}) copy-start(bf16[1,2048,1,8]{1,3,2,0:T(8,128)(2,1)S(1)} %get-tuple-element.91) | copy-start | bytes 98308
  51.0 10.8 %copy-start.27 = (bf16[1,2048,1,8]{1,3,2,0:T(8,128)(2,1)}, bf16[1,2048,1,8]{1,3,2,0:T(8,128)(2,1)S(1)}, u32[]{:S(2)}) copy-start(bf16[1,2048,1,8]{1,3,2,0:T(8,128)(2,1)S(1)} %get-tuple-element.92) | copy-start | bytes 98308
  51.0 10.7 %copy-start.12 = (bf16[1,2048,1,48]{1,3,2,0:T(8,128)(2,1)}, bf16[1,2048,1,48]{1,3,2,0:T(8,128)(2,1)S(1)}, u32[]{:S(2)}) copy-start(bf16[1,2048,1,48]{1,3,2,0:T(8,128)(2,1)S(1)} %slice.387) | copy-start | bytes 589828
  57.2 21.4 %copy-start.10 = (f32[512,3,1024]{2,0,1:T(8,128)}, f32[512,3,1024]{2,0,1:T(8,128)S(1)}, u32[]{:S(2)}) copy-start(f32[512,3,1024]{2,0,1:T(8,128)S(1)} %get-tuple-element.105) | copy-start | bytes 18874372
  61.8 7.4 %copy-start.1 = (f32[512,3,1536]{2,0,1:T(8,128)}, f32[512,3,1536]{2,0,1:T(8,128)S(1)}, u32[]{:S(2)}) copy-start(f32[512,3,1536]{2,0,1:T(8,128)S(1)} %get-tuple-element.107) | copy-start | bytes 28311556
  70.6 8.1 %copy-start.16 = (bf16[1,2048,128]{1,2,0:T(8,128)(2,1)S(1)}, bf16[1,2048,128]{1,2,0:T(8,128)(2,1)}, u32[]{:S(2)}) copy-start(bf16[1,2048,128]{1,2,0:T(8,128)(2,1)} %get-tuple-element.102) | copy-start | bytes 1572868
  70.6 11.6 %slice-start = ((s8[9437184]{0:T(1024)(128)(4,1)}), s8[1048576]{0:T(1024)(128)(4,1)S(1)}, s32[]{:S(2)}) async-start(s8[9437184]{0:T(1024)(128)(4,1)} %bitcast.278), calls=%async_computation.8 | async-start | bytes 2097152
  94.3 7.4 %copy-start.8 = (f32[512,3,512]{0,2,1:T(8,128)S(1)}, f32[512,3,512]{0,2,1:T(8,128)}, u32[]{:S(2)}) copy-start(f32[512,3,512]{0,2,1:T(8,128)} %copy-done.7) | copy-start | bytes 9437188
  94.3 7.4 %copy-start.17 = (bf16[1,2048,128]{1,2,0:T(8,128)(2,1)S(1)}, bf16[1,2048,128]{1,2,0:T(8,128)(2,1)}, u32[]{:S(2)}) copy-start(bf16[1,2048,128]{1,2,0:T(8,128)(2,1)} %get-tuple-element.102) | copy-start | bytes 1572868
  94.3 7.4 %copy-start.47 = (f32[512,3]{0,1:T(4,128)S(1)}, f32[512,3]{0,1:T(4,128)}, u32[]{:S(2)}) copy-start(f32[512,3]{0,1:T(4,128)} %copy-done.46) | copy-start | bytes 18436
  94.3 7.4 %copy-start.49 = (f32[512,3]{0,1:T(4,128)S(1)}, f32[512,3]{0,1:T(4,128)}, u32[]{:S(2)}) copy-start(f32[512,3]{0,1:T(4,128)} %copy-done.48) | copy-start | bytes 18436
  94.3 7.4 %copy-start.67 = (f32[512,3,64]{0,2,1:T(8,128)S(1)}, f32[512,3,64]{0,2,1:T(8,128)}, u32[]{:S(2)}) copy-start(f32[512,3,64]{0,2,1:T(8,128)} %get-tuple-element.118) | copy-start | bytes 1179652
  94.3 7.4 %copy-start.68 = (f32[512,3,64]{0,2,1:T(8,128)S(1)}, f32[512,3,64]{0,2,1:T(8,128)}, u32[]{:S(2)}) copy-start(f32[512,3,64]{0,2,1:T(8,128)} %get-tuple-element.116) | copy-start | bytes 1179652
  94.3 7.4 %copy-start.69 = (f32[512,3,64]{0,2,1:T(8,128)S(1)}, f32[512,3,64]{0,2,1:T(8,128)}, u32[]{:S(2)}) copy-start(f32[512,3,64]{0,2,1:T(8,128)} %get-tuple-element.114) | copy-start | bytes 1179652
  94.4 9.4 %slice-start.9 = ((s8[12582912]{0:T(1024)(128)(4,1)}), s8[4194304]{0:T(1024)(128)(4,1)S(1)}, s32[]{:S(2)}) async-start(s8[12582912]{0:T(1024)(128)(4,1)} %bitcast.284), calls=%async_computation.17 | async-start | bytes 8388608
  94.4 9.4 %slice-start.10 = ((s8[12582912]{0:T(1024)(128)(4,1)}), s8[4194304]{0:T(1024)(128)(4,1)S(1)}, s32[]{:S(2)}) async-start(s8[12582912]{0:T(1024)(128)(4,1)} %bitcast.284), calls=%async_computation.18 | async-start | bytes 8388608
  131.8 16.3 %copy-start.61 = (bf16[1,2048,768]{2,1,0:T(8,128)(2,1)S(1)}, bf16[1,2048,768]{2,1,0:T(8,128)(2,1)}, u32[]{:S(2)}) copy-start(bf16[1,2048,768]{2,1,0:T(8,128)(2,1)} %all-gather.6.cloned.1.call-done) | copy-start | bytes 9437188
  131.8 16.3 %copy-start.62 = (bf16[768,768]{1,0:T(8,128)(2,1)S(1)}, bf16[768,768]{1,0:T(8,128)(2,1)}, u32[]{:S(2)}) copy-start(bf16[768,768]{1,0:T(8,128)(2,1)} %param.31) | copy-start | bytes 3538948
  148.1 9.7 %copy-start.64 = (bf16[2048,768]{1,0:T(8,128)(2,1)}, bf16[2048,768]{1,0:T(8,128)(2,1)S(1)}, u32[]{:S(2)}) copy-start(bf16[2048,768]{1,0:T(8,128)(2,1)S(1)} %get-tuple-element.111) | copy-start | bytes 9437188
  163.2 164.6 %reduce-scatter.5.cloned.1.call-start = ((), (), s32[]{:S(2)}) async-start(), calls=%async_computation.5 | async-start | bytes 3932160 | tf_op jit(solution)/shard_map/reduce_scatter | solution.py:226
  174.0 194.0 %reduce-scatter.3.cloned.1.call-start = ((), (), s32[]{:S(2)}) async-start(), calls=%async_computation.3 | async-start | bytes 3932160 | tf_op jit(solution)/shard_map/reduce_scatter | solution.py:142
  182.0 287.3 %all-gather.8.cloned.1.call-start = ((), (), s32[]{:S(2)}) async-start(), calls=%async_computation.6 | async-start | bytes 13381632 | tf_op jit(solution)/shard_map/all_gather | solution.py:248
  185.9 182.2 %copy-start.11 = (bf16[1,512,768]{2,1,0:T(8,128)(2,1)S(1)}, bf16[1,512,768]{2,1,0:T(8,128)(2,1)}, u32[]{:S(2)}) copy-start(bf16[1,512,768]{2,1,0:T(8,128)(2,1)} %param.24) | copy-start | bytes 2359300
  (58 other events, 199.8 us)
Sparse Core Ops, SparseCore 0:
  9.6 31.2 all-gather.3
  43.0 28.5 all-gather.5
  163.3 124.9 all-reduce.3
  290.9 36.7 reduce-scatter.4
  330.1 37.9 reduce-scatter.2
  371.3 97.9 all-gather.7
